TPU v7x, 512 devices: a whole 4x4x16 slice. The times are simulated.
512 devices in a mesh: dp: 64 (over y, x, z_lo), mp: 8 (over z_hi, core).
Axes of the slice: x: 4, y: 4, z: 16 (z_hi: 4, z_lo: 4; z = z_hi * 4 + z_lo), core: 2. Of those that a mesh axis runs over, the one named last changes fastest.
Arguments:
- normed: bfloat16 [4096, 6144], P('mp', 'dp'), may hold values from -6 to 6
- hidden_cot: bfloat16 [4096, 12288], P('mp', 'dp'), may hold values from -6 to 6
- up_rows: bfloat16 [12288, 6144], P('dp'), may hold values from -0.078125 to 0.078125
Outputs:
- hidden: bfloat16 [4096, 12288], P('mp', 'dp')
- input_grad: bfloat16 [4096, 6144], P('mp', 'dp')
- up_grad: bfloat16 [12288, 6144], P('dp')
All inputs are finite; a program needn't handle non-finite values.
Results may differ from a plain program's by a relative error of at most 0.013.
Values may be sent and summed in bfloat16 or wider, within the bound.
No kernel may reach another device: no remote copies, remote signals or barrier semaphores. Data moves between devices by JAX's collectives and lax.ppermute only.
A program may use at most 64 MiB of HBM per device.

v0:
```python
import jax
import jax.numpy as jnp
from jax import lax
from jax.sharding import PartitionSpec as P

inv_sqrt_two = 0.7071067811865476
inv_sqrt_two_pi = 0.3989422804014327


def gelu_parts(preact):
    normal_cdf = 0.5 * (1.0 + lax.erf(preact * inv_sqrt_two))
    gelu_out = preact * normal_cdf
    gelu_slope = normal_cdf + preact * jnp.exp(-0.5 * preact * preact) * inv_sqrt_two_pi
    return (gelu_out, gelu_slope)


def contract_last(left, right):
    return lax.dot_general(
        left, right, (((1,), (1,)), ((), ())), preferred_element_type=jnp.float32
    )


def contract_first(left, right):
    return lax.dot_general(
        left, right, (((0,), (0,)), ((), ())), preferred_element_type=jnp.float32
    )


def local(normed, hidden_cot, up_rows):
    full_in = lax.all_gather(normed, "dp", axis=1, tiled=True)
    column_rows = lax.all_to_all(up_rows, "dp", split_axis=1, concat_axis=0, tiled=True)
    replicas = lax.axis_size("mp")
    preact = contract_last(full_in, up_rows)
    gelu_out, gelu_slope = gelu_parts(preact)
    hidden = gelu_out.astype(jnp.bfloat16)
    hidden_grad = (hidden_cot.astype(jnp.float32) * gelu_slope).astype(jnp.bfloat16)
    up_term = contract_first(hidden_grad, full_in)
    up_total = lax.psum(up_term.astype(jnp.bfloat16), "mp").astype(jnp.float32)
    up_grad = (up_total / replicas).astype(jnp.bfloat16)
    input_total = jnp.dot(
        lax.all_gather(hidden_grad, "dp", axis=1, tiled=True),
        column_rows,
        preferred_element_type=jnp.float32,
    )
    input_grad = input_total.astype(jnp.bfloat16)
    return (hidden, input_grad, up_grad)


def solution(mesh):
    return jax.shard_map(
        local,
        mesh=mesh,
        in_specs=(P("mp", "dp"), P("mp", "dp"), P("dp", None)),
        out_specs=(P("mp", "dp"), P("mp", "dp"), P("dp", None)),
        check_vma=False,
    )
```

profile of v0, /device:TPU:128, one launch (start us, length us, event | category | flops | bytes accessed | tf_op | source)
XLA Modules:
  0.0 975.7 jit_solution(11073580016380807391)
XLA Ops:
  7.2 0.0 all-gather.3.cloned.1.call-start
  7.2 0.7 all-gather.3.cloned.1.call-update
  7.9 0.0 all-reduce.2.cloned.1.call-start
  7.9 379.4 %all-gather.3.cloned.1.call-done = bf16[512,6144]{0,1:T(8,128)(2,1)} async-done(((bf16[512,96]{0,1:T(8,128)(2,1)}), bf16[512,6144]{0,1:T(8,128)(2,1)}) %all-gather.3.cloned.1.call-update) | async-done | bytes 6291472 | tf_op jit(solution)/shard_map/all_gather | solution.py:30
  387.4 5.7 fusion.5
  393.1 0.0 copy-start
  393.1 6.4 convolution_convert_fusion
  399.5 0.0 copy-done
  399.5 0.0 all-reduce.2.cloned.1.call-update
  399.5 0.0 all-gather.5.cloned.1.call-start
  399.6 0.7 all-gather.5.cloned.1.call-update
  400.3 3.0 copy.7
  403.3 95.6 %all_to_all.19 = bf16[192,64,96]{0,2,1:T(8,128)(2,1)S(1)} all-to-all(bf16[192,64,96]{0,2,1:T(8,128)(2,1)S(1)} %bitcast.11), channel_id=1, replica_groups=mesh['dp'=64,'mp'=8] {'dp'}, dimensions={1} | all-to-all | bytes 4718592 | tf_op jit(solution)/shard_map/all_to_all | solution.py:31
  498.8 3.4 copy.8
  502.3 5.1 all_to_all.17
  507.4 50.8 %all-reduce.2.cloned.1.call-done = bf16[192,6144]{1,0:T(8,128)(2,1)} async-done(((bf16[192,6144]{1,0:T(8,128)(2,1)}), bf16[192,6144]{1,0:T(8,128)(2,1)}) %all-reduce.2.cloned.1.call-update) | async-done | bytes 2359312 | tf_op jit(solution)/shard_map/psum | solution.py:38
  558.2 3.5 multiply_convert_fusion
  561.7 400.1 %all-gather.5.cloned.1.call-done = bf16[512,12288]{0,1:T(8,128)(2,1)} async-done(((bf16[512,192]{0,1:T(8,128)(2,1)}), bf16[512,12288]{0,1:T(8,128)(2,1)}) %all-gather.5.cloned.1.call-update) | async-done | bytes 12582928 | tf_op jit(solution)/shard_map/all_gather | solution.py:41
  961.8 7.3 convolution_convert_fusion.1
Async XLA Ops:
  7.2 380.2 %all-gather.3.cloned.1.call-start = ((), (), s32[]{:S(2)}) async-start(), calls=%async_computation.1 | async-start | bytes 6389760 | tf_op jit(solution)/shard_map/all_gather | solution.py:30
  7.9 550.3 %all-reduce.2.cloned.1.call-start = ((), (), s32[]{:S(2)}) async-start(), calls=%async_computation.3 | async-start | bytes 4718592 | tf_op jit(solution)/shard_map/psum | solution.py:38
  393.1 6.4 copy-start
  399.5 562.3 %all-gather.5.cloned.1.call-start = ((), (), s32[]{:S(2)}) async-start(), calls=%async_computation.2 | async-start | bytes 12779520 | tf_op jit(solution)/shard_map/all_gather | solution.py:41
Sparse Core Ops, SparseCore 0:
  10.0 377.2 all-gather.2
  399.6 158.5 all-reduce.1
  560.3 401.4 all-gather.4
where the time goes:
time: 976 us
  waiting for transfers between devices  832 us (85%)
  blocking collectives  95.6 us (10%)
  matrix products  19.5 us (2%)
  between operations  13.8 us (1%)
  local copies, waits for them, and re-layouts  11.6 us (1%)
    all_gather x1, waiting for transfers between devices, local(): lax.all_gather(hidden_grad, 'dp', axis=1, tiled=True)  400 us
    all_gather x1, waiting for transfers between devices, local(): full_in = lax.all_gather(normed, 'dp', axis=1, tiled=True)  379 us
    all_to_all x1, blocking collectives, local(): lax.all_to_all(up_rows, 'dp', split_axis=1, concat_axis=0, tiled=True)  95.6 us
    psum x1, waiting for transfers between devices, local(): up_total = lax.psum(up_term.astype(jnp.bfloat16), 'mp').astype(jnp.float32)  50.8 us
  transfers between devices with their start and end apart: 3, of which 3 were waited for; matrix products, arithmetic and copies ran while one was open for 1% of the time, Pallas kernels for 0%

commit v1 on v0

--- a/solution.py
+++ b/solution.py
@@ -1,3 +1,4 @@
+import functools
 import jax
 import jax.numpy as jnp
 from jax import lax
@@ -5,6 +6,21 @@
 
 inv_sqrt_two = 0.7071067811865476
 inv_sqrt_two_pi = 0.3989422804014327
+
+
+def serve_zones_now(my_tile, mesh_name):
+    return jnp.concatenate(
+        lax.all_to_all(
+            jnp.stack([my_tile] * lax.axis_size(mesh_name)),
+            axis_name=mesh_name,
+            split_axis=0,
+            concat_axis=0,
+        ),
+        axis=1,
+    )
+
+
+_place_racks = functools.partial(serve_zones_now, mesh_name="dp")
 
 
 def gelu_parts(preact):
@@ -38,9 +54,7 @@
     up_total = lax.psum(up_term.astype(jnp.bfloat16), "mp").astype(jnp.float32)
     up_grad = (up_total / replicas).astype(jnp.bfloat16)
     input_total = jnp.dot(
-        lax.all_gather(hidden_grad, "dp", axis=1, tiled=True),
-        column_rows,
-        preferred_element_type=jnp.float32,
+        _place_racks(hidden_grad), column_rows, preferred_element_type=jnp.float32
     )
     input_grad = input_total.astype(jnp.bfloat16)
     return (hidden, input_grad, up_grad)

time: 976 us -> 758 us (0.78)
  the two profiles are of different devices: /device:TPU:128 before, /device:TPU:32 now
where the time goes in v1:
time: 758 us
  waiting for transfers between devices  688 us (91%)
  starting transfers between devices  22.9 us (3%)
  matrix products  19.4 us (3%)
  between operations  14.1 us (2%)
  local copies, waits for them, and re-layouts  10.5 us (1%)
    all_gather x1, waiting for transfers between devices, local(): full_in = lax.all_gather(normed, 'dp', axis=1, tiled=True)  370 us
    psum x1, waiting for transfers between devices, local(): up_total = lax.psum(up_term.astype(jnp.bfloat16), 'mp').astype(jnp.float32)  260 us
    all_to_all x1, waiting for transfers between devices, serve_zones_now(): lax.all_to_all(jnp.stack([my_tile] * lax.axis_size(mesh_name)), axis_name...  56.9 us
  transfers between devices with their start and end apart: 4, of which 3 were waited for; matrix products, arithmetic and copies ran while one was open for 3% of the time, Pallas kernels for 0%

profile of v1, /device:TPU:32, one launch (start us, length us, event | category | flops | bytes accessed | tf_op | source)
XLA Modules:
  0.0 758.0 jit_solution(6204170049940441262)
XLA Ops:
  7.2 0.0 all-gather.2.cloned.1.call-start
  7.2 0.7 all-gather.2.cloned.1.call-update
  7.9 0.0 copy-start
  7.9 4.5 copy.6
  12.4 11.7 %all-to-all-start.1 = ((bf16[192,64,96]{0,2,1:T(8,128)(2,1)}), bf16[192,64,96]{0,2,1:T(8,128)(2,1)S(1)}, u32[]{:S(2)}, u32[]{:S(2)}) async-start(bf16[192,64,96]{0,2,1:T(8,128)(2,1)} %bitcast.23), calls=%async_computation.1 | async-start | bytes 6291456 | tf_op jit(solution)/shard_map/all_to_all | solution.py:47
  24.1 370.2 %all-gather.2.cloned.1.call-done = bf16[512,6144]{0,1:T(8,128)(2,1)} async-done(((bf16[512,96]{0,1:T(8,128)(2,1)}), bf16[512,6144]{0,1:T(8,128)(2,1)}) %all-gather.2.cloned.1.call-update) | async-done | bytes 6291472 | tf_op jit(solution)/shard_map/all_gather | solution.py:46
  394.3 0.0 copy-done
  394.3 5.7 fusion.18
  400.1 0.0 all-to-all-done.1
  400.1 6.0 stack.2
  406.1 11.2 %all-to-all-start = ((bf16[64,512,192]{1,2,0:T(8,128)(2,1)}), bf16[64,512,192]{1,2,0:T(8,128)(2,1)}, u32[]{:S(2)}, u32[]{:S(2)}) async-start(bf16[64,512,192]{1,2,0:T(8,128)(2,1)} %stack.2), calls=%async_computation | async-start | bytes 25165824 | tf_op jit(solution)/shard_map/all_to_all | solution.py:13
  417.2 0.0 all-reduce.2.cloned.1.call-start
  417.3 6.4 convolution_convert_fusion
  423.7 0.0 all-reduce.2.cloned.1.call-update
  423.7 259.6 %all-reduce.2.cloned.1.call-done = bf16[192,6144]{1,0:T(8,128)(2,1)} async-done(((bf16[192,6144]{1,0:T(8,128)(2,1)}), bf16[192,6144]{1,0:T(8,128)(2,1)}) %all-reduce.2.cloned.1.call-update) | async-done | bytes 2359312 | tf_op jit(solution)/shard_map/psum | solution.py:54
  683.3 3.5 multiply_convert_fusion
  686.9 56.9 %all-to-all-done = bf16[64,512,192]{1,2,0:T(8,128)(2,1)} async-done(((bf16[64,512,192]{1,2,0:T(8,128)(2,1)}), bf16[64,512,192]{1,2,0:T(8,128)(2,1)}, u32[]{:S(2)}, u32[]{:S(2)}) %all-to-all-start) | async-done | bytes 12582944 | tf_op jit(solution)/shard_map/all_to_all | solution.py:13
  743.8 7.4 fusion.8
Async XLA Ops:
  7.2 387.2 %all-gather.2.cloned.1.call-start = ((), (), s32[]{:S(2)}) async-start(), calls=%async_computation.2 | async-start | bytes 6389760 | tf_op jit(solution)/shard_map/all_gather | solution.py:46
  7.9 386.4 %copy-start = (bf16[512,192]{0,1:T(8,128)(2,1)S(1)}, bf16[512,192]{0,1:T(8,128)(2,1)}, u32[]{:S(2)}) copy-start(bf16[512,192]{0,1:T(8,128)(2,1)} %param.4) | copy-start | bytes 589828
  12.4 387.6 %all-to-all-start.1 = ((bf16[192,64,96]{0,2,1:T(8,128)(2,1)}), bf16[192,64,96]{0,2,1:T(8,128)(2,1)S(1)}, u32[]{:S(2)}, u32[]{:S(2)}) async-start(bf16[192,64,96]{0,2,1:T(8,128)(2,1)} %bitcast.23), calls=%async_computation.1 | async-start | bytes 6291456 | tf_op jit(solution)/shard_map/all_to_all | solution.py:47
  406.1 337.8 %all-to-all-start = ((bf16[64,512,192]{1,2,0:T(8,128)(2,1)}), bf16[64,512,192]{1,2,0:T(8,128)(2,1)}, u32[]{:S(2)}, u32[]{:S(2)}) async-start(bf16[64,512,192]{1,2,0:T(8,128)(2,1)} %stack.2), calls=%async_computation | async-start | bytes 25165824 | tf_op jit(solution)/shard_map/all_to_all | solution.py:13
  417.2 266.1 %all-reduce.2.cloned.1.call-start = ((), (), s32[]{:S(2)}) async-start(), calls=%async_computation.3 | async-start | bytes 4718592 | tf_op jit(solution)/shard_map/psum | solution.py:54
Sparse Core Ops, SparseCore 0:
  10.1 384.2 all-gather.1
  423.8 259.4 all-reduce.1
